TPU v7x, 32 devices: a whole 2x2x4 slice. The times are simulated.
32 devices in a mesh: pipe: 4 (over y, x), expert: 8 (over z, core).
Axes of the slice: x: 2, y: 2, z: 4, core: 2. Of those that a mesh axis runs over, the one named last changes fastest.
Arguments:
- activations: bfloat16 [4, 1024, 2560], P('pipe', 'expert'), may hold values from -6 to 6
- out_grad: bfloat16 [4, 1024, 2560], P('pipe', 'expert'), may hold values from -6 to 6
- expert_ids: int32 [4, 1024, 2], P('pipe', 'expert'), may hold values from 0 to 3, all different within a row; in each aligned block of 128 rows (0 to 127, 128 to 255, ..., all dimensions but the last counted through in order) at most 96 rows name the same one
- gate_values: float32 [4, 1024, 2], P('pipe', 'expert'), may hold values from 0.1 to 1
- w_gate: bfloat16 [4, 2560, 3072], P('pipe', None, 'expert'), may hold values from -0.125 to 0.125
- w_up: bfloat16 [4, 2560, 3072], P('pipe', None, 'expert'), may hold values from -0.125 to 0.125
- w_down: bfloat16 [4, 3072, 2560], P('pipe', 'expert'), may hold values from -0.21875 to 0.21875
Outputs:
- passed_grad: bfloat16 [4, 1024, 2560], P('pipe', 'expert')
- router_grad: float32 [4, 1024, 2], P('pipe', 'expert')
Inputs may be any that keep to these rules, and one draw needn't show every extreme that they name: `expert_ids`: each row names 2 different experts. In the 128 rows of one section on one device (aligned blocks of rows) no expert is named by more than 96 rows, a bound that some block reaches; every expert is named somewhere.
All inputs are finite; a program needn't handle non-finite values.
Results may differ from a plain program's by a relative error of at most 0.0095.
Values may be sent and summed in bfloat16 or wider, within the bound.
A program may use at most 128 MiB of HBM per device.

v0:
```python
import jax
import jax.numpy as jnp
from jax import lax
from jax.sharding import PartitionSpec as P


def shifted(block, axis, distance):
    devices = range(lax.axis_size(axis))
    route = [(i - distance, i) for i in devices if i - distance in devices]
    return lax.ppermute(block, axis, route)


def expert_terms(rows_in, rows_grad, gate_cols, up_cols, down_rows):
    contract = (((1,), (1,)), ((), ()))
    gate_pre = jnp.dot(rows_in, gate_cols, preferred_element_type=jnp.float32)
    up_pre = jnp.dot(rows_in, up_cols, preferred_element_type=jnp.float32)
    squash = jax.nn.sigmoid(gate_pre)
    activated = gate_pre * squash
    hidden = (activated * up_pre).astype(jnp.bfloat16)
    back_hidden = lax.dot_general(
        rows_grad, down_rows, contract, preferred_element_type=jnp.float32
    )
    router_part = jnp.sum(hidden.astype(jnp.float32) * back_hidden, axis=1)
    slope = squash * (1.0 + gate_pre * (1.0 - squash))
    grad_gate = (back_hidden * up_pre * slope).astype(jnp.bfloat16)
    grad_up = (back_hidden * activated).astype(jnp.bfloat16)
    route_part = lax.dot_general(grad_gate, gate_cols, contract, preferred_element_type=jnp.float32)
    route_part = route_part + lax.dot_general(
        grad_up, up_cols, contract, preferred_element_type=jnp.float32
    )
    return (route_part, router_part)


def local(activations, out_grad, expert_ids, gate_values, w_gate, w_up, w_down):
    inputs = activations[0]
    grads_out = out_grad[0]
    routes = expert_ids[0]
    weights_gate = gate_values[0]
    gate_local = w_gate[0]
    up_local = w_up[0]
    down_local = w_down[0]
    devices_e = lax.axis_size("expert")
    owners = devices_e // 2
    tokens_dev, top_k = routes.shape
    feat_width = inputs.shape[1]
    capacity = min(tokens_dev * 3 // 4, tokens_dev * top_k * 3 // (2 * owners))
    count_entries = tokens_dev * top_k
    flat_ids = routes.reshape(-1)
    one_hot = (flat_ids[:, None] == jnp.arange(owners, dtype=jnp.int32)[None, :]).astype(jnp.int32)
    slot_rank = jnp.sum((jnp.cumsum(one_hot, axis=0) - 1) * one_hot, axis=1)
    slot_index = flat_ids * capacity + slot_rank
    slot_table = (
        jnp.full((owners * capacity,), count_entries, jnp.int32)
        .at[slot_index]
        .set(jnp.arange(count_entries, dtype=jnp.int32))
    )
    token_of = slot_table // top_k
    pad_row = jnp.zeros((1, feat_width), inputs.dtype)
    send_in = jnp.concatenate([inputs, pad_row], 0)[token_of].reshape(owners, capacity, feat_width)
    send_grad = jnp.concatenate([grads_out, pad_row], 0)[token_of].reshape(
        owners, capacity, feat_width
    )
    full_in = lax.all_to_all(
        jnp.repeat(send_in, 2, axis=0), "expert", split_axis=0, concat_axis=0, tiled=True
    )
    item_count = full_in.shape[1]
    route_part, router_part = expert_terms(
        full_in.reshape(-1, feat_width),
        lax.all_to_all(
            jnp.repeat(send_grad, 2, axis=0), "expert", split_axis=0, concat_axis=0, tiled=True
        ).reshape(-1, feat_width),
        gate_local,
        up_local,
        down_local,
    )
    route_part = route_part.reshape(devices_e, item_count, feat_width)
    router_part = router_part.reshape(devices_e, item_count)
    back_route = lax.all_to_all(
        route_part.astype(jnp.bfloat16), "expert", split_axis=0, concat_axis=0, tiled=True
    ).astype(route_part.dtype)
    back_router = lax.all_to_all(
        router_part.astype(jnp.bfloat16), "expert", split_axis=0, concat_axis=0, tiled=True
    ).astype(router_part.dtype)
    summed = jnp.sum(back_route.reshape(owners, 2, item_count, feat_width), axis=1)
    router_sum = jnp.sum(back_router.reshape(owners, 2, item_count), axis=1)
    route_sum, router_sum = (summed, router_sum)
    entry_route = route_sum.reshape(-1, feat_width)[slot_index]
    entry_router = router_sum.reshape(-1)[slot_index]
    input_grad = jnp.sum(
        weights_gate.reshape(tokens_dev, top_k, 1)
        * entry_route.reshape(tokens_dev, top_k, feat_width),
        axis=1,
    ).astype(jnp.bfloat16)
    passed = shifted(input_grad, "pipe", -1)
    return (passed[None], entry_router.reshape(tokens_dev, top_k)[None])


def solution(mesh):
    return jax.shard_map(
        local,
        mesh=mesh,
        in_specs=(
            P("pipe", "expert", None),
            P("pipe", "expert", None),
            P("pipe", "expert", None),
            P("pipe", "expert", None),
            P("pipe", None, "expert"),
            P("pipe", None, "expert"),
            P("pipe", "expert", None),
        ),
        out_specs=(P("pipe", "expert", None), P("pipe", "expert", None)),
        check_vma=False,
    )
```

profile of v0, /device:TPU:0, one launch (start us, length us, event | category | flops | bytes accessed | tf_op | source)
XLA Modules:
  0.0 350.7 jit_solution(5297020244395157370)
XLA Ops:
  0.6 0.0 copy-start
  0.6 0.9 copy.21
  1.6 0.1 eq.29
  1.7 0.1 eq.25
  1.9 0.7 broadcast_multiply_fusion
  2.5 1.2 reduce-window.6
  3.8 0.1 slice.16
  3.8 0.1 copy.23
  4.0 0.1 copy.24
  4.1 0.1 add_bitcast_fusion
  4.1 0.1 copy.20
  4.3 0.1 mul.57
  4.4 1.4 scatter_custom_fusion
  5.9 1.1 concatenate.7
  7.0 3.3 gather_fusion.1
  10.3 3.8 %broadcast_in_dim.24 = bf16[4,2,96,2560]{3,2,1,0:T(8,128)(2,1)} broadcast(bf16[4,96,2560]{2,1,0:T(8,128)(2,1)} %bitcast.56), dimensions={0,2,3} | broadcast | bytes 5898240 | tf_op jit(solution)/shard_map/broadcast_in_dim | solution.py:64
  14.1 0.0 copy-start.4
  14.1 6.5 %all-to-all-start.1 = ((bf16[8,96,2560]{2,1,0:T(8,128)(2,1)}), bf16[8,96,2560]{2,1,0:T(8,128)(2,1)}, u32[]{:S(2)}, u32[]{:S(2)}) async-start(bf16[8,96,2560]{2,1,0:T(8,128)(2,1)} %bitcast.52), calls=%async_computation.1 | async-start | bytes 7864320 | tf_op jit(solution)/shard_map/all_to_all | solution.py:63
  20.6 0.0 copy-done.4
  20.6 3.3 gather_fusion
  23.9 85.1 %all-to-all-done.1 = bf16[8,96,2560]{2,1,0:T(8,128)(2,1)} async-done(((bf16[8,96,2560]{2,1,0:T(8,128)(2,1)}), bf16[8,96,2560]{2,1,0:T(8,128)(2,1)}, u32[]{:S(2)}, u32[]{:S(2)}) %all-to-all-start.1) | async-done | bytes 3932192 | tf_op jit(solution)/shard_map/all_to_all | solution.py:63
  109.0 3.8 %broadcast_in_dim.23 = bf16[4,2,96,2560]{3,2,1,0:T(8,128)(2,1)} broadcast(bf16[4,96,2560]{2,1,0:T(8,128)(2,1)} %bitcast.55), dimensions={0,2,3} | broadcast | bytes 5898240 | tf_op jit(solution)/shard_map/broadcast_in_dim | solution.py:70
  112.8 4.7 %all-to-all-start = ((bf16[8,96,2560]{2,1,0:T(8,128)(2,1)}), bf16[8,96,2560]{2,1,0:T(8,128)(2,1)}, u32[]{:S(2)}, u32[]{:S(2)}) async-start(bf16[8,96,2560]{2,1,0:T(8,128)(2,1)} %bitcast.53), calls=%async_computation | async-start | bytes 7864320 | tf_op jit(solution)/shard_map/all_to_all | solution.py:69
  117.5 0.0 copy-done
  117.6 0.0 copy-start.2
  117.6 4.0 %fusion.2 = f32[768,384]{0,1:T(8,128)S(1)} fusion(bf16[768,2560]{1,0:T(8,128)(2,1)} %bitcast.13, bf16[1,2560,384]{2,1,0:T(8,128)(2,1)S(1)} %copy-done), kind=kOutput, calls=%fused_computation.10 | convolution fusion | flops 1509949440 | bytes 7077888 | tf_op jit(solution)/shard_map/dot_general | solution.py:15
  121.6 0.0 copy-done.2
  121.6 4.9 %fusion.5 = f32[768,384]{0,1:T(8,128)} fusion(bf16[768,2560]{1,0:T(8,128)(2,1)} %bitcast.13, bf16[1,2560,384]{2,1,0:T(8,128)(2,1)S(1)} %copy-done.2), kind=kOutput, calls=%fused_computation.13 | convolution fusion | flops 1509949440 | bytes 7077888 | tf_op jit(solution)/shard_map/dot_general | solution.py:16
  126.5 79.3 %all-to-all-done = bf16[8,96,2560]{2,1,0:T(8,128)(2,1)} async-done(((bf16[8,96,2560]{2,1,0:T(8,128)(2,1)}), bf16[8,96,2560]{2,1,0:T(8,128)(2,1)}, u32[]{:S(2)}, u32[]{:S(2)}) %all-to-all-start) | async-done | bytes 3932192 | tf_op jit(solution)/shard_map/all_to_all | solution.py:69
  205.7 0.0 copy-start.1
  205.7 4.9 %multiply_reduce_fusion.1 = (bf16[768]{0:T(1024)(128)(2,1)S(1)}, f32[768,384]{0,1:T(8,128)S(1)}) fusion(f32[768,384]{0,1:T(8,128)} %fusion.5, f32[768,384]{0,1:T(8,128)S(1)} %fusion.2, bf16[768,2560]{1,0:T(8,128)(2,1)} %bitcast.8, bf16[1,384,2560]{2,1,0:T(8,128)(2,1)} %param.13), kind=kOutput, calls=%fused_computation.17 | convolution fusion | flops 1512602880 | bytes 9438720 | tf_op jit(solution)/shard_map/dot_general | solution.py:20
  210.6 0.0 copy-done.1
  210.7 0.0 copy-start.3
  210.7 2.5 fusion
  213.1 0.0 copy-done.3
  213.1 4.3 %add_convert_fusion = bf16[768,2560]{1,0:T(8,128)(2,1)} fusion(f32[768,2560]{1,0:T(8,128)S(1)} %fusion, bf16[1,2560,384]{2,1,0:T(8,128)(2,1)S(1)} %copy-done.3, f32[768,384]{0,1:T(8,128)S(1)} %get-tuple-element.7, f32[768,384]{0,1:T(8,128)S(1)} %fusion.2), kind=kOutput, calls=%fused_computation.6 | convolution fusion | flops 1515651072 | bytes 16121856 | tf_op jit(solution)/shard_map/dot_general | solution.py:28
  217.4 0.0 copy-start.5
  217.4 4.9 %all-to-all-start.2 = ((bf16[8,96,2560]{2,1,0:T(8,128)(2,1)}), bf16[8,96,2560]{2,1,0:T(8,128)(2,1)}, u32[]{:S(2)}, u32[]{:S(2)}) async-start(bf16[8,96,2560]{2,1,0:T(8,128)(2,1)} %bitcast.54), calls=%async_computation.2 | async-start | bytes 7864320 | tf_op jit(solution)/shard_map/all_to_all | solution.py:78
  222.3 0.0 copy-done.5
  222.3 0.1 copy.19
  222.4 88.0 %all-to-all-done.2 = bf16[8,96,2560]{2,1,0:T(8,128)(2,1)} async-done(((bf16[8,96,2560]{2,1,0:T(8,128)(2,1)}), bf16[8,96,2560]{2,1,0:T(8,128)(2,1)}, u32[]{:S(2)}, u32[]{:S(2)}) %all-to-all-start.2) | async-done | bytes 3932192 | tf_op jit(solution)/shard_map/all_to_all | solution.py:78
  310.4 5.2 %convert_reduce_fusion = f32[4,96,2560]{2,1,0:T(8,128)} fusion(bf16[8,96,2560]{2,1,0:T(8,128)(2,1)} %all-to-all-done.2), kind=kLoop, calls=%fused_computation.5 | loop fusion | flops 2949120 | bytes 7864320 | tf_op jit(solution)/shard_map/reduce_sum | solution.py:84
  315.7 6.2 %gather_fusion.2 = f32[256,2560]{1,0:T(8,128)} fusion(f32[384,2560]{1,0:T(8,128)} %bitcast.51, s32[1024]{0:T(1024)S(1)} %pad_clamp_fusion), kind=kCustom, calls=%fused_computation.2 | custom fusion | bytes 5243904 | tf_op jit(solution)/shard_map/gather | solution.py:87
  321.9 4.4 %reshape.115 = f32[128,2,2560]{2,1,0:T(2,128)} reshape(f32[256,2560]{1,0:T(8,128)} %gather_fusion.2) | data formatting | bytes 5242880 | tf_op jit(solution)/shard_map/reshape | solution.py:91
  326.3 5.5 %multiply_reduce_fusion = bf16[128,2560]{1,0:T(8,128)(2,1)S(1)} fusion(f32[128,2,2560]{2,1,0:T(2,128)} %reshape.115, f32[128,2]{1,0:T(8,128)S(1)} %copy.19), kind=kLoop, calls=%fused_computation.7 | loop fusion | flops 983040 | bytes 3277824 | tf_op jit(solution)/shard_map/reduce_sum | solution.py:89
  331.8 1.3 collective-permute-start
  333.1 0.1 convert_element_type.64
  333.2 7.9 %all_to_all.21 = bf16[8,1,96]{2,1,0:T(2,128)(2,1)S(1)} all-to-all(bf16[8,1,96]{2,1,0:T(2,128)(2,1)S(1)} %convert_element_type.64), channel_id=1, replica_groups=mesh['pipe'=4,'expert'=8] {'expert'}, dimensions={0} | all-to-all | bytes 3072 | tf_op jit(solution)/shard_map/all_to_all | solution.py:81
  341.1 0.1 reshape.116
  341.2 1.9 gather_fusion.3
  343.2 0.1 broadcast_in_dim_reshape.3
  343.3 0.6 copy.26
  344.0 5.9 %collective-permute-done = bf16[128,2560]{1,0:T(8,128)(2,1)S(1)} collective-permute-done((bf16[128,2560]{1,0:T(8,128)(2,1)S(1)}, bf16[128,2560]{1,0:T(8,128)(2,1)S(1)}, u32[]{:S(2)}, u32[]{:S(2)}) %collective-permute-start) | collective-permute-done | bytes 655392 | tf_op jit(solution)/shard_map/ppermute | solution.py:10
  349.9 0.8 copy.30
  (12 shorter events, 0.2 us)
Async XLA Ops:
  0.6 116.9 %copy-start = (bf16[1,2560,384]{2,1,0:T(8,128)(2,1)S(1)}, bf16[1,2560,384]{2,1,0:T(8,128)(2,1)}, u32[]{:S(2)}) copy-start(bf16[1,2560,384]{2,1,0:T(8,128)(2,1)} %param.11) | copy-start | bytes 5898244
  14.1 6.5 %copy-start.4 = (bf16[1,128,2560]{2,1,0:T(8,128)(2,1)S(1)}, bf16[1,128,2560]{2,1,0:T(8,128)(2,1)}, u32[]{:S(2)}) copy-start(bf16[1,128,2560]{2,1,0:T(8,128)(2,1)} %param.8) | copy-start | bytes 1966084
  14.1 94.9 %all-to-all-start.1 = ((bf16[8,96,2560]{2,1,0:T(8,128)(2,1)}), bf16[8,96,2560]{2,1,0:T(8,128)(2,1)}, u32[]{:S(2)}, u32[]{:S(2)}) async-start(bf16[8,96,2560]{2,1,0:T(8,128)(2,1)} %bitcast.52), calls=%async_computation.1 | async-start | bytes 7864320 | tf_op jit(solution)/shard_map/all_to_all | solution.py:63
  112.8 92.9 %all-to-all-start = ((bf16[8,96,2560]{2,1,0:T(8,128)(2,1)}), bf16[8,96,2560]{2,1,0:T(8,128)(2,1)}, u32[]{:S(2)}, u32[]{:S(2)}) async-start(bf16[8,96,2560]{2,1,0:T(8,128)(2,1)} %bitcast.53), calls=%async_computation | async-start | bytes 7864320 | tf_op jit(solution)/shard_map/all_to_all | solution.py:69
  117.6 4.0 %copy-start.2 = (bf16[1,2560,384]{2,1,0:T(8,128)(2,1)S(1)}, bf16[1,2560,384]{2,1,0:T(8,128)(2,1)}, u32[]{:S(2)}) copy-start(bf16[1,2560,384]{2,1,0:T(8,128)(2,1)} %param.12) | copy-start | bytes 5898244
  205.7 4.9 %copy-start.1 = (f32[768,384]{0,1:T(8,128)S(1)}, f32[768,384]{0,1:T(8,128)}, u32[]{:S(2)}) copy-start(f32[768,384]{0,1:T(8,128)} %fusion.5) | copy-start | bytes 3538948
  210.7 2.5 copy-start.3
  217.4 4.9 %copy-start.5 = (f32[1,128,2]{1,2,0:T(2,128)S(1)}, f32[1,128,2]{1,2,0:T(2,128)}, u32[]{:S(2)}) copy-start(f32[1,128,2]{1,2,0:T(2,128)} %param.10) | copy-start | bytes 3076
  217.4 93.0 %all-to-all-start.2 = ((bf16[8,96,2560]{2,1,0:T(8,128)(2,1)}), bf16[8,96,2560]{2,1,0:T(8,128)(2,1)}, u32[]{:S(2)}, u32[]{:S(2)}) async-start(bf16[8,96,2560]{2,1,0:T(8,128)(2,1)} %bitcast.54), calls=%async_computation.2 | async-start | bytes 7864320 | tf_op jit(solution)/shard_map/all_to_all | solution.py:78
  331.8 18.1 %collective-permute-start = (bf16[128,2560]{1,0:T(8,128)(2,1)S(1)}, bf16[128,2560]{1,0:T(8,128)(2,1)S(1)}, u32[]{:S(2)}, u32[]{:S(2)}) collective-permute-start(bf16[128,2560]{1,0:T(8,128)(2,1)S(1)} %multiply_reduce_fusion), channel_id=1, source_target_pairs={{8,0},{16,8},{24,16},{9,1},{17,9},{25,17},{10,2},{18,10},{26,18},{... | collective-permute-start | bytes 1966088 | tf_op jit(solution)/shard_map/ppermute | solution.py:10
where the time goes:
time: 351 us
  waiting for transfers between devices  258 us (74%)
  local copies, waits for them, and re-layouts  32.9 us (9%)
  matrix products  20.5 us (6%)
  starting transfers between devices  17.4 us (5%)
  other arithmetic  12.8 us (4%)
  blocking collectives  7.94 us (2%)
    all_to_all x1, waiting for transfers between devices, local(): lax.all_to_all(route_part.astype(jnp.bfloat16), 'expert', split_axis=0, c...  88 us
    all_to_all x1, waiting for transfers between devices, local(): lax.all_to_all(jnp.repeat(send_in, 2, axis=0), 'expert', split_axis=0, co...  85.1 us
    all_to_all x1, waiting for transfers between devices, local(): lax.all_to_all(jnp.repeat(send_grad, 2, axis=0), 'expert', split_axis=0,...  79.3 us
    all_to_all x1, blocking collectives, local(): lax.all_to_all(router_part.astype(jnp.bfloat16), 'expert', split_axis=0,...  7.94 us
  transfers between devices with their start and end apart: 4, of which 4 were waited for; matrix products, arithmetic and copies ran while one was open for 4% of the time, Pallas kernels for 0%

commit v1 on v0

--- a/solution.py
+++ b/solution.py
@@ -2,6 +2,22 @@
 import jax.numpy as jnp
 from jax import lax
 from jax.sharding import PartitionSpec as P
+
+
+def pairwise_exchange(shard, axis, split, join):
+    ways, here = (lax.axis_size(axis), lax.axis_index(axis))
+    width = shard.shape[split] // ways
+    shape = list(shard.shape)
+    shape[split] = width
+    height = shape[join]
+    shape[join] = height * ways
+    full = jnp.zeros(shape, shard.dtype)
+    for mask in range(ways):
+        part = lax.dynamic_slice_in_dim(shard, (here ^ mask) * width, width, axis=split)
+        if mask:
+            part = lax.ppermute(part, axis, [(d, d ^ mask) for d in range(ways)])
+        full = lax.dynamic_update_slice_in_dim(full, part, (here ^ mask) * height, axis=join)
+    return full
 
 
 def shifted(block, axis, distance):
@@ -60,9 +76,7 @@
     send_grad = jnp.concatenate([grads_out, pad_row], 0)[token_of].reshape(
         owners, capacity, feat_width
     )
-    full_in = lax.all_to_all(
-        jnp.repeat(send_in, 2, axis=0), "expert", split_axis=0, concat_axis=0, tiled=True
-    )
+    full_in = pairwise_exchange(jnp.repeat(send_in, 2, axis=0), "expert", 0, 0)
     item_count = full_in.shape[1]
     route_part, router_part = expert_terms(
         full_in.reshape(-1, feat_width),

time: 351 us -> 341 us (0.972)
  waiting for transfers between devices: 258 us -> 229 us
  starting transfers between devices: 17.4 us -> 41.9 us
  matrix products: 20.5 us -> 16.2 us
    ppermute x0 -> x7, waiting for transfers between devices: none -> 134 us  [pairwise_exchange(): part = lax.ppermute(part, axis, [(d, d ^ mask) for d in range(ways)])]
    all_to_all x1 -> x0, waiting for transfers between devices: 85.1 us -> none  [local(): lax.all_to_all(jnp.repeat(send_in, 2, axis=0), 'expert', split_axis=0, co...]
    all_to_all x1, waiting for transfers between devices: 79.3 us -> 0.01 us  [local(): lax.all_to_all(jnp.repeat(send_grad, 2, axis=0), 'expert', split_axis=0,...]
    all_to_all x1, starting transfers between devices: 4.86 us -> 23.3 us  [local(): lax.all_to_all(route_part.astype(jnp.bfloat16), 'expert', split_axis=0, c...]
    ppermute x0 -> x7, starting transfers between devices: none -> 10.8 us  [pairwise_exchange(): part = lax.ppermute(part, axis, [(d, d ^ mask) for d in range(ways)])]
    all_to_all x1 -> x0, starting transfers between devices: 6.49 us -> none  [local(): lax.all_to_all(jnp.repeat(send_in, 2, axis=0), 'expert', split_axis=0, co...]
  transfers between devices with their start and end apart: 4 -> 10, of which waited for: 4 -> 6; matrix products, arithmetic and copies ran while one was open for 4% -> 4% of each run, Pallas kernels for 0% -> 0%
where the time goes in v1:
time: 341 us; the launch traced here: 340 us
  waiting for transfers between devices  229 us (67%)
  starting transfers between devices  41.9 us (12%)
  local copies, waits for them, and re-layouts  32 us (9%)
  matrix products  16.2 us (5%)
  other arithmetic  12.8 us (4%)
  blocking collectives  7.94 us (2%)
    ppermute x7, waiting for transfers between devices, pairwise_exchange(): part = lax.ppermute(part, axis, [(d, d ^ mask) for d in range(ways)])  134 us
    all_to_all x1, waiting for transfers between devices, local(): lax.all_to_all(route_part.astype(jnp.bfloat16), 'expert', split_axis=0, c...  88.8 us
    all_to_all x1, starting transfers between devices, local(): lax.all_to_all(route_part.astype(jnp.bfloat16), 'expert', split_axis=0, c...  23.3 us
    ppermute x7, starting transfers between devices, pairwise_exchange(): part = lax.ppermute(part, axis, [(d, d ^ mask) for d in range(ways)])  10.8 us
    all_to_all x1, blocking collectives, local(): lax.all_to_all(router_part.astype(jnp.bfloat16), 'expert', split_axis=0,...  7.94 us
  transfers between devices with their start and end apart: 10, of which 6 were waited for; matrix products, arithmetic and copies ran while one was open for 4% of the time, Pallas kernels for 0%

profile of v1, /device:TPU:0, one launch (start us, length us, event | category | flops | bytes accessed | tf_op | source)
XLA Modules:
  0.0 340.5 jit_solution(13140686146567877030)
XLA Ops:
  0.6 0.0 copy-start
  0.6 0.9 copy.21
  1.6 0.1 eq.29
  1.7 0.1 eq.25
  1.9 0.7 broadcast_multiply_fusion
  2.5 1.2 reduce-window.6
  3.8 0.1 slice.16
  3.8 0.1 copy.23
  4.0 0.1 copy.24
  4.1 0.1 add_bitcast_fusion
  4.1 0.1 copy.20
  4.3 0.1 mul.57
  4.4 1.4 scatter_custom_fusion
  5.9 1.1 concatenate.6
  7.0 3.3 gather_fusion
  10.3 3.8 %broadcast_in_dim.26 = bf16[4,2,96,2560]{3,2,1,0:T(8,128)(2,1)} broadcast(bf16[4,96,2560]{2,1,0:T(8,128)(2,1)} %bitcast.56), dimensions={0,2,3} | broadcast | bytes 5898240 | tf_op jit(solution)/shard_map/broadcast_in_dim | solution.py:84
  14.1 6.5 %all-to-all-start = ((bf16[8,96,2560]{2,1,0:T(8,128)(2,1)}), bf16[8,96,2560]{2,1,0:T(8,128)(2,1)}, u32[]{:S(2)}, u32[]{:S(2)}) async-start(bf16[8,96,2560]{2,1,0:T(8,128)(2,1)} %bitcast.53), calls=%async_computation | async-start | bytes 7864320 | tf_op jit(solution)/shard_map/all_to_all | solution.py:83
  20.5 0.0 copy-done.4
  20.6 3.3 gather_fusion.1
  23.9 1.9 broadcast_in_dim.28
  25.8 0.3 broadcast_in_dim.27
  26.1 0.4 constant_dynamic-slice_fusion
  26.5 0.6 collective-permute-start
  27.1 1.6 collective-permute-start.1
  28.7 0.0 collective-permute-start.2
  28.7 2.6 collective-permute-start.3
  31.4 0.1 collective-permute-start.4
  31.5 0.0 collective-permute-done
  31.5 3.4 %collective-permute-start.5 = (bf16[1,96,2560]{2,1,0:T(8,128)(2,1)S(1)}, bf16[1,96,2560]{2,1,0:T(8,128)(2,1)S(1)}, u32[]{:S(2)}, u32[]{:S(2)}) collective-permute-start(bf16[1,96,2560]{2,1,0:T(8,128)(2,1)S(1)} %get-tuple-element.7), channel_id=1, source_target_pairs={{0,6},{1,7},{2,4},{3,5},{4,2},{5,3},{6,0},{7,1},{8,14},{9,15},{10,... | collective-permute-start | bytes 1474568 | tf_op jit(solution)/shard_map/ppermute | solution.py:18
  35.0 60.7 %collective-permute-done.1 = bf16[1,96,2560]{2,1,0:T(8,128)(2,1)S(1)} collective-permute-done((bf16[1,96,2560]{2,1,0:T(8,128)(2,1)S(1)}, bf16[1,96,2560]{2,1,0:T(8,128)(2,1)S(1)}, u32[]{:S(2)}, u32[]{:S(2)}) %collective-permute-start.1) | collective-permute-done | bytes 491552 | tf_op jit(solution)/shard_map/ppermute | solution.py:18
  95.6 2.4 collective-permute-start.6
  98.1 8.0 %collective-permute-done.2 = bf16[1,96,2560]{2,1,0:T(8,128)(2,1)S(1)} collective-permute-done((bf16[1,96,2560]{2,1,0:T(8,128)(2,1)S(1)}, bf16[1,96,2560]{2,1,0:T(8,128)(2,1)S(1)}, u32[]{:S(2)}, u32[]{:S(2)}) %collective-permute-start.2) | collective-permute-done | bytes 491552 | tf_op jit(solution)/shard_map/ppermute | solution.py:18
  106.2 56.0 %collective-permute-done.3 = bf16[1,96,2560]{2,1,0:T(8,128)(2,1)S(1)} collective-permute-done((bf16[1,96,2560]{2,1,0:T(8,128)(2,1)S(1)}, bf16[1,96,2560]{2,1,0:T(8,128)(2,1)S(1)}, u32[]{:S(2)}, u32[]{:S(2)}) %collective-permute-start.3) | collective-permute-done | bytes 491552 | tf_op jit(solution)/shard_map/ppermute | solution.py:18
  162.2 9.3 %collective-permute-done.4 = bf16[1,96,2560]{2,1,0:T(8,128)(2,1)S(1)} collective-permute-done((bf16[1,96,2560]{2,1,0:T(8,128)(2,1)S(1)}, bf16[1,96,2560]{2,1,0:T(8,128)(2,1)S(1)}, u32[]{:S(2)}, u32[]{:S(2)}) %collective-permute-start.4) | collective-permute-done | bytes 491552 | tf_op jit(solution)/shard_map/ppermute | solution.py:18
  171.6 0.0 collective-permute-done.5
  171.6 0.0 collective-permute-done.6
  171.7 0.0 copy-done
  171.7 0.0 copy-start.2
  171.7 1.7 fusion.2
  173.4 0.0 copy-done.2
  173.5 2.9 fusion.5
  176.3 0.0 all-to-all-done
  176.3 4.9 %multiply_reduce_fusion.1 = (bf16[768]{0:T(1024)(128)(2,1)S(1)}, f32[768,384]{0,1:T(8,128)S(1)}) fusion(f32[768,384]{0,1:T(8,128)} %fusion.5, f32[768,384]{0,1:T(8,128)S(1)} %fusion.2, bf16[768,2560]{1,0:T(8,128)(2,1)} %bitcast.8, bf16[1,384,2560]{2,1,0:T(8,128)(2,1)} %param.13), kind=kOutput, calls=%fused_computation.17 | convolution fusion | flops 1512602880 | bytes 9438720 | tf_op jit(solution)/shard_map/dot_general | solution.py:36
  181.2 0.0 copy-done.1
  181.2 0.0 copy-start.3
  181.3 2.5 fusion
  183.7 0.0 copy-done.3
  183.7 4.3 %add_convert_fusion = bf16[768,2560]{1,0:T(8,128)(2,1)} fusion(f32[768,2560]{1,0:T(8,128)S(1)} %fusion, bf16[1,2560,384]{2,1,0:T(8,128)(2,1)S(1)} %copy-done.3, f32[768,384]{0,1:T(8,128)S(1)} %get-tuple-element.15, f32[768,384]{0,1:T(8,128)S(1)} %fusion.2), kind=kOutput, calls=%fused_computation.6 | convolution fusion | flops 1515651072 | bytes 16121856 | tf_op jit(solution)/shard_map/dot_general | solution.py:44
  188.0 23.3 %all-to-all-start.1 = ((bf16[8,96,2560]{2,1,0:T(8,128)(2,1)}), bf16[8,96,2560]{2,1,0:T(8,128)(2,1)}, u32[]{:S(2)}, u32[]{:S(2)}) async-start(bf16[8,96,2560]{2,1,0:T(8,128)(2,1)} %bitcast.54), calls=%async_computation.1 | async-start | bytes 7864320 | tf_op jit(solution)/shard_map/all_to_all | solution.py:92
  211.3 0.1 copy.19
  211.5 88.8 %all-to-all-done.1 = bf16[8,96,2560]{2,1,0:T(8,128)(2,1)} async-done(((bf16[8,96,2560]{2,1,0:T(8,128)(2,1)}), bf16[8,96,2560]{2,1,0:T(8,128)(2,1)}, u32[]{:S(2)}, u32[]{:S(2)}) %all-to-all-start.1) | async-done | bytes 3932192 | tf_op jit(solution)/shard_map/all_to_all | solution.py:92
  300.2 5.2 %convert_reduce_fusion = f32[4,96,2560]{2,1,0:T(8,128)} fusion(bf16[8,96,2560]{2,1,0:T(8,128)(2,1)} %all-to-all-done.1), kind=kLoop, calls=%fused_computation.5 | loop fusion | flops 2949120 | bytes 7864320 | tf_op jit(solution)/shard_map/reduce_sum | solution.py:98
  305.5 6.2 %gather_fusion.2 = f32[256,2560]{1,0:T(8,128)} fusion(f32[384,2560]{1,0:T(8,128)} %bitcast.51, s32[1024]{0:T(1024)S(1)} %pad_clamp_fusion), kind=kCustom, calls=%fused_computation.2 | custom fusion | bytes 5243904 | tf_op jit(solution)/shard_map/gather | solution.py:101
  311.7 4.4 %reshape.115 = f32[128,2,2560]{2,1,0:T(2,128)} reshape(f32[256,2560]{1,0:T(8,128)} %gather_fusion.2) | data formatting | bytes 5242880 | tf_op jit(solution)/shard_map/reshape | solution.py:105
  316.1 5.5 %multiply_reduce_fusion = bf16[128,2560]{1,0:T(8,128)(2,1)S(1)} fusion(f32[128,2,2560]{2,1,0:T(2,128)} %reshape.115, f32[128,2]{1,0:T(8,128)S(1)} %copy.19), kind=kLoop, calls=%fused_computation.7 | loop fusion | flops 983040 | bytes 3277824 | tf_op jit(solution)/shard_map/reduce_sum | solution.py:103
  321.6 1.3 collective-permute-start.7
  322.9 0.1 convert_element_type.64
  323.0 7.9 %all_to_all.16 = bf16[8,1,96]{2,1,0:T(2,128)(2,1)S(1)} all-to-all(bf16[8,1,96]{2,1,0:T(2,128)(2,1)S(1)} %convert_element_type.64), channel_id=1, replica_groups=mesh['pipe'=4,'expert'=8] {'expert'}, dimensions={0} | all-to-all | bytes 3072 | tf_op jit(solution)/shard_map/all_to_all | solution.py:95
  330.9 0.1 reshape.116
  331.0 1.9 gather_fusion.3
  333.0 0.1 broadcast_in_dim_reshape.3
  333.1 0.6 copy.26
  333.8 5.9 %collective-permute-done.7 = bf16[128,2560]{1,0:T(8,128)(2,1)S(1)} collective-permute-done((bf16[128,2560]{1,0:T(8,128)(2,1)S(1)}, bf16[128,2560]{1,0:T(8,128)(2,1)S(1)}, u32[]{:S(2)}, u32[]{:S(2)}) %collective-permute-start.7) | collective-permute-done | bytes 655392 | tf_op jit(solution)/shard_map/ppermute | solution.py:26
  339.7 0.8 copy.38
  (23 shorter events, 0.4 us)
Async XLA Ops:
  0.6 171.1 %copy-start = (bf16[1,2560,384]{2,1,0:T(8,128)(2,1)S(1)}, bf16[1,2560,384]{2,1,0:T(8,128)(2,1)}, u32[]{:S(2)}) copy-start(bf16[1,2560,384]{2,1,0:T(8,128)(2,1)} %param.11) | copy-start | bytes 5898244
  14.1 6.5 %copy-start.4 = (bf16[1,128,2560]{2,1,0:T(8,128)(2,1)S(1)}, bf16[1,128,2560]{2,1,0:T(8,128)(2,1)}, u32[]{:S(2)}) copy-start(bf16[1,128,2560]{2,1,0:T(8,128)(2,1)} %param.7) | copy-start | bytes 1966084
  14.1 162.3 %all-to-all-start = ((bf16[8,96,2560]{2,1,0:T(8,128)(2,1)}), bf16[8,96,2560]{2,1,0:T(8,128)(2,1)}, u32[]{:S(2)}, u32[]{:S(2)}) async-start(bf16[8,96,2560]{2,1,0:T(8,128)(2,1)} %bitcast.53), calls=%async_computation | async-start | bytes 7864320 | tf_op jit(solution)/shard_map/all_to_all | solution.py:83
  26.5 5.0 %collective-permute-start = (bf16[1,96,2560]{2,1,0:T(8,128)(2,1)S(1)}, bf16[1,96,2560]{2,1,0:T(8,128)(2,1)S(1)}, u32[]{:S(2)}, u32[]{:S(2)}) collective-permute-start(bf16[1,96,2560]{2,1,0:T(8,128)(2,1)S(1)} %get-tuple-element.12), channel_id=1, source_target_pairs={{0,1},{1,0},{2,3},{3,2},{4,5},{5,4},{6,7},{7,6},{8,9},{9,8},{10,11... | collective-permute-start | bytes 1474568 | tf_op jit(solution)/shard_map/ppermute | solution.py:18
  27.1 68.5 %collective-permute-start.1 = (bf16[1,96,2560]{2,1,0:T(8,128)(2,1)S(1)}, bf16[1,96,2560]{2,1,0:T(8,128)(2,1)S(1)}, u32[]{:S(2)}, u32[]{:S(2)}) collective-permute-start(bf16[1,96,2560]{2,1,0:T(8,128)(2,1)S(1)} %get-tuple-element.11), channel_id=1, source_target_pairs={{0,2},{1,3},{2,0},{3,1},{4,6},{5,7},{6,4},{7,5},{8,10},{9,11},{10,... | collective-permute-start | bytes 1474568 | tf_op jit(solution)/shard_map/ppermute | solution.py:18
  28.7 77.4 %collective-permute-start.2 = (bf16[1,96,2560]{2,1,0:T(8,128)(2,1)S(1)}, bf16[1,96,2560]{2,1,0:T(8,128)(2,1)S(1)}, u32[]{:S(2)}, u32[]{:S(2)}) collective-permute-start(bf16[1,96,2560]{2,1,0:T(8,128)(2,1)S(1)} %get-tuple-element.10), channel_id=1, source_target_pairs={{0,3},{1,2},{2,1},{3,0},{4,7},{5,6},{6,5},{7,4},{8,11},{9,10},{10,... | collective-permute-start | bytes 1474568 | tf_op jit(solution)/shard_map/ppermute | solution.py:18
  28.7 133.4 %collective-permute-start.3 = (bf16[1,96,2560]{2,1,0:T(8,128)(2,1)S(1)}, bf16[1,96,2560]{2,1,0:T(8,128)(2,1)S(1)}, u32[]{:S(2)}, u32[]{:S(2)}) collective-permute-start(bf16[1,96,2560]{2,1,0:T(8,128)(2,1)S(1)} %get-tuple-element.9), channel_id=1, source_target_pairs={{0,4},{1,5},{2,6},{3,7},{4,0},{5,1},{6,2},{7,3},{8,12},{9,13},{10,... | collective-permute-start | bytes 1474568 | tf_op jit(solution)/shard_map/ppermute | solution.py:18
  31.4 140.2 %collective-permute-start.4 = (bf16[1,96,2560]{2,1,0:T(8,128)(2,1)S(1)}, bf16[1,96,2560]{2,1,0:T(8,128)(2,1)S(1)}, u32[]{:S(2)}, u32[]{:S(2)}) collective-permute-start(bf16[1,96,2560]{2,1,0:T(8,128)(2,1)S(1)} %get-tuple-element.8), channel_id=1, source_target_pairs={{0,5},{1,4},{2,7},{3,6},{4,1},{5,0},{6,3},{7,2},{8,13},{9,12},{10,... | collective-permute-start | bytes 1474568 | tf_op jit(solution)/shard_map/ppermute | solution.py:18
  31.5 140.1 %collective-permute-start.5 = (bf16[1,96,2560]{2,1,0:T(8,128)(2,1)S(1)}, bf16[1,96,2560]{2,1,0:T(8,128)(2,1)S(1)}, u32[]{:S(2)}, u32[]{:S(2)}) collective-permute-start(bf16[1,96,2560]{2,1,0:T(8,128)(2,1)S(1)} %get-tuple-element.7), channel_id=1, source_target_pairs={{0,6},{1,7},{2,4},{3,5},{4,2},{5,3},{6,0},{7,1},{8,14},{9,15},{10,... | collective-permute-start | bytes 1474568 | tf_op jit(solution)/shard_map/ppermute | solution.py:18
  95.6 76.0 %collective-permute-start.6 = (bf16[1,96,2560]{2,1,0:T(8,128)(2,1)S(1)}, bf16[1,96,2560]{2,1,0:T(8,128)(2,1)S(1)}, u32[]{:S(2)}, u32[]{:S(2)}) collective-permute-start(bf16[1,96,2560]{2,1,0:T(8,128)(2,1)S(1)} %get-tuple-element.6), channel_id=1, source_target_pairs={{0,7},{1,6},{2,5},{3,4},{4,3},{5,2},{6,1},{7,0},{8,15},{9,14},{10,... | collective-permute-start | bytes 1474568 | tf_op jit(solution)/shard_map/ppermute | solution.py:18
  171.7 1.8 copy-start.2
  176.3 4.9 %copy-start.1 = (f32[768,384]{0,1:T(8,128)S(1)}, f32[768,384]{0,1:T(8,128)}, u32[]{:S(2)}) copy-start(f32[768,384]{0,1:T(8,128)} %fusion.5) | copy-start | bytes 3538948
  181.2 2.5 copy-start.3
  188.0 23.3 %copy-start.5 = (f32[1,128,2]{1,2,0:T(2,128)S(1)}, f32[1,128,2]{1,2,0:T(2,128)}, u32[]{:S(2)}) copy-start(f32[1,128,2]{1,2,0:T(2,128)} %param.10) | copy-start | bytes 3076
  188.0 112.2 %all-to-all-start.1 = ((bf16[8,96,2560]{2,1,0:T(8,128)(2,1)}), bf16[8,96,2560]{2,1,0:T(8,128)(2,1)}, u32[]{:S(2)}, u32[]{:S(2)}) async-start(bf16[8,96,2560]{2,1,0:T(8,128)(2,1)} %bitcast.54), calls=%async_computation.1 | async-start | bytes 7864320 | tf_op jit(solution)/shard_map/all_to_all | solution.py:92
  321.6 18.1 %collective-permute-start.7 = (bf16[128,2560]{1,0:T(8,128)(2,1)S(1)}, bf16[128,2560]{1,0:T(8,128)(2,1)S(1)}, u32[]{:S(2)}, u32[]{:S(2)}) collective-permute-start(bf16[128,2560]{1,0:T(8,128)(2,1)S(1)} %multiply_reduce_fusion), channel_id=1, source_target_pairs={{8,0},{16,8},{24,16},{9,1},{17,9},{25,17},{10,2},{18,10},{26,18},{... | collective-permute-start | bytes 1966088 | tf_op jit(solution)/shard_map/ppermute | solution.py:26
